TPU v7x, 512 devices: a whole 4x8x8 slice. The times are simulated.
512 devices in a mesh: expert: 16 (over z, core), tensor: 32 (over x, y).
Axes of the slice: x: 4, y: 8, z: 8, core: 2. Of those that a mesh axis runs over, the one named last changes fastest.
Arguments:
- tokens: bfloat16 [2048, 5120], P('expert', 'tensor'), may hold values from -6 to 6
- routes: int32 [2048, 6], P('expert'), may hold values from 0 to 15, all different within a row; in each aligned block of 128 rows (0 to 127, 128 to 255, ...) at most 64 rows name the same one
- gates: float32 [2048, 6], P('expert'), may hold values from 0.05 to 0.35
- w_gate: bfloat16 [16, 1536, 5120], P('expert', 'tensor'), may hold values from -0.078125 to 0.078125
- w_up: bfloat16 [16, 1536, 5120], P('expert', 'tensor'), may hold values from -0.078125 to 0.078125
- w_down: bfloat16 [16, 1536, 5120], P('expert', None, 'tensor'), may hold values from -0.15625 to 0.15625
- shared_gate: bfloat16 [1536, 5120], P('tensor'), may hold values from -0.078125 to 0.078125
- shared_up: bfloat16 [1536, 5120], P('tensor'), may hold values from -0.078125 to 0.078125
- shared_down: bfloat16 [1536, 5120], P(None, 'tensor'), may hold values from -0.15625 to 0.15625
- vocab: bfloat16 [65536, 5120], P(('expert', 'tensor'))
- targets: int32 [64], replicated, may hold values from 0 to 65535
Outputs:
- layer_out: bfloat16 [2048, 5120], P('expert', 'tensor')
- loglik: float32 [64], replicated
Inputs may be any that keep to these rules, and one draw needn't show every extreme that they name: `routes`: the tokens of one group name one expert at most 64 times; in every draw some group names some expert exactly 64 times.
All inputs are finite; a program needn't handle non-finite values.
Results may differ from a plain program's by a relative error of at most 0.0041.
Values may be sent and summed in bfloat16 or wider, within the bound.
No kernel may reach another device: no remote copies, remote signals or barrier semaphores. Data moves between devices by JAX's collectives and lax.ppermute only.
A program may use at most 64 MiB of HBM per device.

v0:
```python
import jax
import jax.numpy as jnp
from jax import lax
from jax.sharding import PartitionSpec as P

EXPERTS = 16
SCORE_E = 4


def slot_tables(routes, gates, capacity):
    picks = (routes[:, :, None] == jnp.arange(EXPERTS, dtype=jnp.int32)[None, None, :]).astype(
        jnp.int32
    )
    per_token = jnp.sum(picks, axis=1)
    earlier = jnp.cumsum(per_token, axis=0) - per_token
    slots = jnp.sum(picks * earlier[:, None, :], axis=2)
    places = (slots[:, :, None] == jnp.arange(capacity, dtype=jnp.int32)[None, None, :]).astype(
        jnp.float32
    )
    picked = picks.astype(jnp.float32)
    select = jnp.einsum("ikr,iks->rsi", picked, places, precision=lax.Precision.HIGHEST)
    weigh = jnp.einsum("ikr,iks,ik->rsi", picked, places, gates, precision=lax.Precision.HIGHEST)
    return (select.astype(jnp.bfloat16), weigh)


def contract_last(left, right):
    return lax.dot_general(
        left, right, (((1,), (1,)), ((), ())), preferred_element_type=jnp.float32
    )


def shards(
    tokens, routes, gates, w_gate, w_up, w_down, shared_gate, shared_up, shared_down, vocab, targets
):
    tok_rows = tokens.shape[0]
    capacity = tok_rows // 2
    groups = lax.axis_size("expert")
    lanes = lax.axis_size("tensor")
    exp_dev = w_gate.shape[0]
    width = w_gate.shape[1]
    out_width = w_down.shape[2]
    select, weigh = slot_tables(routes, gates, capacity)
    outgoing = jnp.einsum("rsi,id->rsd", select, tokens, preferred_element_type=jnp.float32).astype(
        jnp.bfloat16
    )
    arrived = lax.all_to_all(outgoing, "expert", split_axis=0, concat_axis=1, tiled=True)
    slot_count = arrived.shape[1]
    flat_rows = arrived.reshape(exp_dev * slot_count, arrived.shape[2])
    pieces = (
        lax.all_gather(flat_rows, "tensor", axis=1, tiled=True),
        lax.all_gather(tokens, "tensor", axis=1, tiled=True),
    )
    span = pieces[0].shape[1]
    rows = pieces[0].reshape(exp_dev, slot_count, span)
    gate_acc = jnp.einsum("erw,efw->erf", rows, w_gate, preferred_element_type=jnp.float32)
    up_acc = jnp.einsum("erw,efw->erf", rows, w_up, preferred_element_type=jnp.float32)
    shared_gate_acc = contract_last(pieces[1], shared_gate)
    shared_up_acc = contract_last(pieces[1], shared_up)
    hidden_routed = (jax.nn.silu(gate_acc) * up_acc).astype(jnp.bfloat16)
    hidden_shared = (jax.nn.silu(shared_gate_acc) * shared_up_acc).astype(jnp.bfloat16)
    flat_hidden = hidden_routed.reshape(exp_dev * slot_count, width)
    pieces = (
        lax.all_gather(flat_hidden, "tensor", axis=1, tiled=True),
        lax.all_gather(hidden_shared, "tensor", axis=1, tiled=True),
    )
    span = pieces[0].shape[1]
    rows = pieces[0].reshape(exp_dev, slot_count, span)
    routed_out = jnp.einsum("erw,ewd->erd", rows, w_down, preferred_element_type=jnp.float32)
    shared_out = jnp.dot(pieces[1], shared_down, preferred_element_type=jnp.float32)
    returned = lax.all_to_all(
        routed_out.astype(jnp.bfloat16), "expert", split_axis=1, concat_axis=0, tiled=True
    )
    routed = jnp.einsum(
        "rsi,rsd->id", weigh, returned.astype(jnp.float32), precision=lax.Precision.HIGHEST
    )
    layer_out = (tokens.astype(jnp.float32) + shared_out + routed).astype(jnp.bfloat16)
    scored = layer_out[tok_rows - SCORE_E :].reshape(1, SCORE_E * out_width)
    collected = lax.all_gather(scored, ("expert", "tensor"), axis=0, tiled=True)
    full_rows = (
        collected.reshape(groups, lanes, SCORE_E, out_width)
        .transpose(0, 2, 1, 3)
        .reshape(groups * SCORE_E, lanes * out_width)
    )
    logits = contract_last(full_rows, vocab)
    exp_sums = jnp.sum(jnp.exp(logits), axis=1)
    offset = (lax.axis_index("expert") * lanes + lax.axis_index("tensor")) * vocab.shape[0]
    columns = offset + jnp.arange(vocab.shape[0], dtype=jnp.int32)
    target_part = jnp.sum(jnp.where(targets[:, None] == columns[None, :], logits, 0.0), axis=1)
    totals, target_logit = lax.psum((exp_sums, target_part), ("expert", "tensor"))
    loglik = target_logit - jnp.log(totals)
    return (layer_out, loglik)


def solution(mesh):
    placed = (
        P("expert", "tensor"),
        P("expert", None),
        P("expert", None),
        P("expert", "tensor", None),
        P("expert", "tensor", None),
        P("expert", None, "tensor"),
        P("tensor", None),
        P("tensor", None),
        P(None, "tensor"),
        P(("expert", "tensor"), None),
        P(),
    )
    return jax.shard_map(
        shards, mesh=mesh, in_specs=placed, out_specs=(P("expert", "tensor"), P()), check_vma=False
    )
```

profile of v0, /device:TPU:1, one launch (start us, length us, event | category | flops | bytes accessed | tf_op | source)
XLA Modules:
  0.0 622.9 jit_solution(7036797286087049021)
XLA Ops:
  7.2 0.0 copy-start
  7.2 0.0 all-gather.7.cloned.1.call-start
  7.2 0.9 copy.21
  8.1 0.3 convert_reduce_fusion
  8.4 0.2 reduce_window_sum.11
  8.6 2.4 select_reduce_fusion
  11.0 1.2 fusion
  12.2 0.3 convolution_convert_fusion.1
  12.6 29.1 %all_to_all.21 = bf16[16,64,160]{2,1,0:T(8,128)(2,1)S(1)} all-to-all(bf16[16,64,160]{2,1,0:T(8,128)(2,1)S(1)} %convolution_convert_fusion.1), channel_id=1, replica_groups=mesh['expert'=16,'tensor'=32] {'expert'}, dimensions={0} | all-to-all | bytes 655360 | tf_op jit(solution)/shard_map/all_to_all | solution.py:46
  41.7 0.9 copy.24
  42.6 0.0 all-gather.7.cloned.1.call-update
  42.6 0.0 all-gather.9.cloned.1.call-start
  42.7 110.4 %all-gather.7.cloned.1.call-done = bf16[1024,5120]{0,1:T(8,128)(2,1)} async-done(((bf16[1024,160]{0,1:T(8,128)(2,1)}), bf16[1024,5120]{0,1:T(8,128)(2,1)}) %all-gather.7.cloned.1.call-update) | async-done | bytes 10485776 | tf_op jit(solution)/shard_map/all_gather | solution.py:50
  153.1 6.1 fusion.11
  159.2 0.9 copy-done.1
  160.0 2.6 fusion.2
  162.7 0.0 all-gather.9.cloned.1.call-update
  162.7 0.2 all-gather.5.cloned.1.call-start
  162.9 0.5 all-gather.5.cloned.1.call-update
  163.5 0.1 copy.22
  163.6 2.7 convolution_bitcast_fusion
  166.3 76.0 %all-gather.9.cloned.1.call-done = bf16[1024,1536]{0,1:T(8,128)(2,1)} async-done(((bf16[1024,48]{0,1:T(8,128)(2,1)}), bf16[1024,1536]{0,1:T(8,128)(2,1)}) %all-gather.9.cloned.1.call-update) | async-done | bytes 3145744 | tf_op jit(solution)/shard_map/all_gather | solution.py:63
  242.3 2.6 fusion.1
  244.9 0.8 copy.25
  245.8 0.5 broadcast.28
  246.3 4.0 reduce.1
  250.3 1.5 reshape.84
  251.8 11.8 %all-to-all-start.1 = ((bf16[16,2,5120]{2,1,0:T(2,128)(2,1)}), bf16[16,2,5120]{2,1,0:T(2,128)(2,1)S(1)}, u32[]{:S(2)}, u32[]{:S(2)}) async-start(bf16[16,2,5120]{2,1,0:T(2,128)(2,1)} %reshape.84), calls=%async_computation.1 | async-start | bytes 655360 | tf_op jit(solution)/shard_map/all_to_all | solution.py:70
  263.6 60.0 %all-gather.5.cloned.1.call-done = bf16[128,5120]{0,1:T(8,128)(2,1)} async-done(((bf16[128,160]{0,1:T(8,128)(2,1)}), bf16[128,5120]{0,1:T(8,128)(2,1)}) %all-gather.5.cloned.1.call-update) | async-done | bytes 1310736 | tf_op jit(solution)/shard_map/all_gather | solution.py:51
  323.6 1.8 fusion.21
  325.3 0.4 fusion.5
  325.7 36.5 %all_gather.16 = bf16[128,1536]{0,1:T(8,128)(2,1)S(1)} all-gather(bf16[128,48]{0,1:T(8,128)(2,1)S(1)} %fusion.5), channel_id=1, replica_groups=mesh['expert'=16,'tensor'=32] {'tensor'}, dimensions={1}, use_global_device_ids=true | all-gather | bytes 405504 | tf_op jit(solution)/shard_map/all_gather | solution.py:64
  362.2 0.9 reshape.85
  363.2 0.1 copy.32
  363.2 1.1 copy-done.5
  364.3 1.1 convolution_bitcast_fusion.1
  365.5 0.3 fusion.4
  365.8 0.1 slice.4
  365.9 0.1 copy.29
  366.0 0.1 reshape.76
  366.1 145.7 %all-gather = bf16[512,1,640]{2,1,0:T(2,128)(2,1)S(1)} all-gather(bf16[1,1,640]{2,1,0:T(2,128)(2,1)S(1)} %reshape.76), channel_id=1, replica_groups=mesh['expert'=16,'tensor'=32] {'expert','tensor'}, dimensions={0}, use_global_device_ids=true | all-gather | bytes 656640 | tf_op jit(solution)/shard_map/all_gather | solution.py:78
  511.8 4.0 reduce
  515.8 0.7 reshape.74
  516.5 0.2 copy.30
  516.7 1.7 reshape.75
  518.4 0.7 exponential_reduce_fusion
  519.1 96.8 %all-reduce = (f32[64]{0:T(128)S(1)}, f32[64]{0:T(128)S(1)}) all-reduce(f32[64]{0:T(128)S(1)} %get-tuple-element.3, f32[64]{0:T(128)S(1)} %get-tuple-element.2), channel_id=1, replica_groups=mesh['expert'=16,'tensor'=32] {'expert','tensor'}, use_global_device_ids=true, to_apply=%region_4.5 | all-reduce | flops 128 | bytes 1024 | tf_op jit(solution)/shard_map/psum | solution.py:89
  615.9 0.5 log_subtract_fusion
  (30 shorter events, 0.1 us)
Async XLA Ops:
  7.2 511.2 %copy-start = (bf16[128,5120]{1,0:T(8,128)(2,1)S(1)}, bf16[128,5120]{1,0:T(8,128)(2,1)}, u32[]{:S(2)}) copy-start(bf16[128,5120]{1,0:T(8,128)(2,1)} %param.20) | copy-start | bytes 3932164
  7.2 145.9 %all-gather.7.cloned.1.call-start = ((), (), s32[]{:S(2)}) async-start(), calls=%async_computation.3 | async-start | bytes 10813440 | tf_op jit(solution)/shard_map/all_gather | solution.py:50
  8.4 3.8 copy-start.10
  12.6 140.5 %copy-start.3 = (bf16[1,48,5120]{2,1,0:T(8,128)(2,1)S(1)}, bf16[1,48,5120]{2,1,0:T(8,128)(2,1)}, u32[]{:S(2)}) copy-start(bf16[1,48,5120]{2,1,0:T(8,128)(2,1)} %param.14) | copy-start | bytes 1474564
  42.6 116.5 %copy-start.4 = (bf16[1,48,5120]{2,1,0:T(8,128)(2,1)S(1)}, bf16[1,48,5120]{2,1,0:T(8,128)(2,1)}, u32[]{:S(2)}) copy-start(bf16[1,48,5120]{2,1,0:T(8,128)(2,1)} %param.15) | copy-start | bytes 1474564
  42.6 199.7 %all-gather.9.cloned.1.call-start = ((), (), s32[]{:S(2)}) async-start(), calls=%async_computation.4 | async-start | bytes 3244032 | tf_op jit(solution)/shard_map/all_gather | solution.py:63
  153.1 7.0 %copy-start.1 = (bf16[1024,5120]{0,1:T(8,128)(2,1)S(1)}, bf16[1024,5120]{0,1:T(8,128)(2,1)}, u32[]{:S(2)}) copy-start(bf16[1024,5120]{0,1:T(8,128)(2,1)} %all-gather.7.cloned.1.call-done) | copy-start | bytes 31457284
  160.0 3.4 copy-start.13
  162.7 160.8 %all-gather.5.cloned.1.call-start = ((), (), s32[]{:S(2)}) async-start(), calls=%async_computation.2 | async-start | bytes 1351680 | tf_op jit(solution)/shard_map/all_gather | solution.py:51
  163.6 78.8 %copy-start.8 = (bf16[1,1536,160]{1,2,0:T(8,128)(2,1)S(1)}, bf16[1,1536,160]{1,2,0:T(8,128)(2,1)}, u32[]{:S(2)}) copy-start(bf16[1,1536,160]{1,2,0:T(8,128)(2,1)} %param.16) | copy-start | bytes 1474564
  250.3 73.2 %copy-start.6 = (bf16[48,5120]{1,0:T(8,128)(2,1)S(1)}, bf16[48,5120]{1,0:T(8,128)(2,1)}, u32[]{:S(2)}) copy-start(bf16[48,5120]{1,0:T(8,128)(2,1)} %param.17) | copy-start | bytes 1474564
  251.8 73.5 %copy-start.7 = (bf16[48,5120]{1,0:T(8,128)(2,1)S(1)}, bf16[48,5120]{1,0:T(8,128)(2,1)}, u32[]{:S(2)}) copy-start(bf16[48,5120]{1,0:T(8,128)(2,1)} %param.18) | copy-start | bytes 1474564
  251.8 110.4 %all-to-all-start.1 = ((bf16[16,2,5120]{2,1,0:T(2,128)(2,1)}), bf16[16,2,5120]{2,1,0:T(2,128)(2,1)S(1)}, u32[]{:S(2)}, u32[]{:S(2)}) async-start(bf16[16,2,5120]{2,1,0:T(2,128)(2,1)} %reshape.84), calls=%async_computation.1 | async-start | bytes 655360 | tf_op jit(solution)/shard_map/all_to_all | solution.py:70
  323.6 1.8 copy-start.2
  363.1 1.2 copy-start.5
  363.1 2.4 copy-start.9
  363.1 2.4 copy-start.11
  365.8 150.0 %copy-start.12 = (bf16[128,160]{0,1:T(8,128)(2,1)}, bf16[128,160]{0,1:T(8,128)(2,1)S(1)}, u32[]{:S(2)}) copy-start(bf16[128,160]{0,1:T(8,128)(2,1)S(1)} %fusion.4) | copy-start | bytes 122884
  516.7 1.7 copy-start.14
Sparse Core Ops, SparseCore 0:
  42.7 110.3 all-gather.6
  162.8 79.4 all-gather.8
  245.5 78.0 all-gather.4
where the time goes:
time: 623 us
  blocking collectives  308 us (49%)
  waiting for transfers between devices  247 us (40%)
  matrix products  19.8 us (3%)
  between operations  14.1 us (2%)
  starting transfers between devices  12.1 us (2%)
  other arithmetic  11.4 us (2%)
  local copies, waits for them, and re-layouts  10.7 us (2%)
    all_gather x1, blocking collectives, shards(): collected = lax.all_gather(scored, ('expert', 'tensor'), axis=0, tiled=True)  146 us
    all_gather x1, waiting for transfers between devices, shards(): lax.all_gather(flat_rows, 'tensor', axis=1, tiled=True)  110 us
    psum x1, blocking collectives, shards(): lax.psum((exp_sums, target_part), ('expert', 'tensor'))  96.8 us
    all_gather x1, waiting for transfers between devices, shards(): lax.all_gather(flat_hidden, 'tensor', axis=1, tiled=True)  76 us
    all_gather x1, waiting for transfers between devices, shards(): lax.all_gather(tokens, 'tensor', axis=1, tiled=True)  60 us
    all_gather x1, blocking collectives, shards(): lax.all_gather(hidden_shared, 'tensor', axis=1, tiled=True)  36.5 us
    all_to_all x1, blocking collectives, shards(): lax.all_to_all(outgoing, 'expert', split_axis=0, concat_axis=1, tiled=True)  29.1 us
  transfers between devices with their start and end apart: 4, of which 3 were waited for; matrix products, arithmetic and copies ran while one was open for 2% of the time, Pallas kernels for 0%

commit v1 on v0

--- a/solution.py
+++ b/solution.py
@@ -86,7 +86,7 @@
     offset = (lax.axis_index("expert") * lanes + lax.axis_index("tensor")) * vocab.shape[0]
     columns = offset + jnp.arange(vocab.shape[0], dtype=jnp.int32)
     target_part = jnp.sum(jnp.where(targets[:, None] == columns[None, :], logits, 0.0), axis=1)
-    totals, target_logit = lax.psum((exp_sums, target_part), ("expert", "tensor"))
+    totals, target_logit = lax.psum(lax.psum((exp_sums, target_part), "tensor"), "expert")
     loglik = target_logit - jnp.log(totals)
     return (layer_out, loglik)
 

time: 623 us -> 623 us (level)
    psum x1 -> x2, blocking collectives: 96.8 us -> 96.2 us  [the longest x1 58.4 us: shards(): lax.psum((exp_sums, target_part), 'tensor')]
where the time goes in v1:
time: 623 us; the launch traced here: 622 us
  blocking collectives  307 us (49%)
  waiting for transfers between devices  247 us (40%)
  matrix products  19.8 us (3%)
  between operations  14.1 us (2%)
  starting transfers between devices  12.1 us (2%)
  other arithmetic  11.4 us (2%)
  local copies, waits for them, and re-layouts  10.7 us (2%)
    all_gather x1, blocking collectives, shards(): collected = lax.all_gather(scored, ('expert', 'tensor'), axis=0, tiled=True)  146 us
    all_gather x1, waiting for transfers between devices, shards(): lax.all_gather(flat_rows, 'tensor', axis=1, tiled=True)  110 us
    all_gather x1, waiting for transfers between devices, shards(): lax.all_gather(flat_hidden, 'tensor', axis=1, tiled=True)  76 us
    all_gather x1, waiting for transfers between devices, shards(): lax.all_gather(tokens, 'tensor', axis=1, tiled=True)  59.9 us
    psum x1, blocking collectives, shards(): lax.psum((exp_sums, target_part), 'tensor')  58.4 us
    psum x1, blocking collectives, shards(): lax.psum(lax.psum((exp_sums, target_part), 'tensor'), 'expert')  37.9 us
    all_gather x1, blocking collectives, shards(): lax.all_gather(hidden_shared, 'tensor', axis=1, tiled=True)  36.5 us
    all_to_all x1, blocking collectives, shards(): lax.all_to_all(outgoing, 'expert', split_axis=0, concat_axis=1, tiled=True)  29.1 us
  transfers between devices with their start and end apart: 4, of which 3 were waited for; matrix products, arithmetic and copies ran while one was open for 2% of the time, Pallas kernels for 0%

profile of v1, /device:TPU:1, one launch (start us, length us, event | category | flops | bytes accessed | tf_op | source)
XLA Modules:
  0.0 622.4 jit_solution(5646233910121018349)
XLA Ops:
  7.2 0.0 all-gather.7.cloned.1.call-start
  7.2 0.9 copy.21
  8.1 0.3 convert_reduce_fusion
  8.4 0.2 reduce_window_sum.11
  8.6 2.4 select_reduce_fusion
  11.0 1.2 fusion
  12.2 0.3 convolution_convert_fusion.1
  12.6 29.1 %all_to_all.21 = bf16[16,64,160]{2,1,0:T(8,128)(2,1)S(1)} all-to-all(bf16[16,64,160]{2,1,0:T(8,128)(2,1)S(1)} %convolution_convert_fusion.1), channel_id=1, replica_groups=mesh['expert'=16,'tensor'=32] {'expert'}, dimensions={0} | all-to-all | bytes 655360 | tf_op jit(solution)/shard_map/all_to_all | solution.py:46
  41.7 0.9 copy.24
  42.6 0.0 all-gather.7.cloned.1.call-update
  42.6 0.0 all-gather.9.cloned.1.call-start
  42.7 110.4 %all-gather.7.cloned.1.call-done = bf16[1024,5120]{0,1:T(8,128)(2,1)} async-done(((bf16[1024,160]{0,1:T(8,128)(2,1)}), bf16[1024,5120]{0,1:T(8,128)(2,1)}) %all-gather.7.cloned.1.call-update) | async-done | bytes 10485776 | tf_op jit(solution)/shard_map/all_gather | solution.py:50
  153.1 6.1 fusion.11
  159.2 0.9 copy-done.1
  160.1 2.6 fusion.2
  162.7 0.0 all-gather.9.cloned.1.call-update
  162.7 0.2 all-gather.5.cloned.1.call-start
  163.0 0.5 all-gather.5.cloned.1.call-update
  163.5 0.1 copy.22
  163.6 2.7 convolution_bitcast_fusion
  166.4 76.0 %all-gather.9.cloned.1.call-done = bf16[1024,1536]{0,1:T(8,128)(2,1)} async-done(((bf16[1024,48]{0,1:T(8,128)(2,1)}), bf16[1024,1536]{0,1:T(8,128)(2,1)}) %all-gather.9.cloned.1.call-update) | async-done | bytes 3145744 | tf_op jit(solution)/shard_map/all_gather | solution.py:63
  242.4 2.6 fusion.1
  244.9 0.8 copy.25
  245.8 0.5 broadcast.28
  246.3 4.0 reduce.1
  250.4 1.5 reshape.84
  251.9 11.8 %all-to-all-start.1 = ((bf16[16,2,5120]{2,1,0:T(2,128)(2,1)}), bf16[16,2,5120]{2,1,0:T(2,128)(2,1)S(1)}, u32[]{:S(2)}, u32[]{:S(2)}) async-start(bf16[16,2,5120]{2,1,0:T(2,128)(2,1)} %reshape.84), calls=%async_computation.1 | async-start | bytes 655360 | tf_op jit(solution)/shard_map/all_to_all | solution.py:70
  263.6 59.9 %all-gather.5.cloned.1.call-done = bf16[128,5120]{0,1:T(8,128)(2,1)} async-done(((bf16[128,160]{0,1:T(8,128)(2,1)}), bf16[128,5120]{0,1:T(8,128)(2,1)}) %all-gather.5.cloned.1.call-update) | async-done | bytes 1310736 | tf_op jit(solution)/shard_map/all_gather | solution.py:51
  323.6 1.8 fusion.21
  325.4 0.4 fusion.5
  325.7 36.5 %all_gather.16 = bf16[128,1536]{0,1:T(8,128)(2,1)S(1)} all-gather(bf16[128,48]{0,1:T(8,128)(2,1)S(1)} %fusion.5), channel_id=1, replica_groups=mesh['expert'=16,'tensor'=32] {'tensor'}, dimensions={1}, use_global_device_ids=true | all-gather | bytes 405504 | tf_op jit(solution)/shard_map/all_gather | solution.py:64
  362.2 0.9 reshape.85
  363.2 0.1 copy.32
  363.3 1.1 copy-done.5
  364.4 1.1 convolution_bitcast_fusion.1
  365.5 0.3 fusion.4
  365.8 0.1 slice.4
  365.9 0.1 copy.29
  366.0 0.1 reshape.76
  366.1 145.7 %all-gather = bf16[512,1,640]{2,1,0:T(2,128)(2,1)S(1)} all-gather(bf16[1,1,640]{2,1,0:T(2,128)(2,1)S(1)} %reshape.76), channel_id=1, replica_groups=mesh['expert'=16,'tensor'=32] {'expert','tensor'}, dimensions={0}, use_global_device_ids=true | all-gather | bytes 656640 | tf_op jit(solution)/shard_map/all_gather | solution.py:78
  511.8 4.0 reduce
  515.8 0.7 reshape.74
  516.5 0.2 copy.30
  516.7 1.7 reshape.75
  518.4 0.7 exponential_reduce_fusion
  519.1 58.4 %all-reduce = (f32[64]{0:T(128)S(1)}, f32[64]{0:T(128)S(1)}) all-reduce(f32[64]{0:T(128)S(1)} %get-tuple-element.3, f32[64]{0:T(128)S(1)} %get-tuple-element.2), channel_id=1, replica_groups=mesh['expert'=16,'tensor'=32] {'tensor'}, use_global_device_ids=true, to_apply=%region_4.5 | all-reduce | flops 128 | bytes 1024 | tf_op jit(solution)/shard_map/psum | solution.py:89
  577.5 37.9 %all-reduce.1 = (f32[64]{0:T(128)S(1)}, f32[64]{0:T(128)S(1)}) all-reduce(f32[64]{0:T(128)S(1)} %get-tuple-element.4, f32[64]{0:T(128)S(1)} %get-tuple-element.5), channel_id=1, replica_groups=mesh['expert'=16,'tensor'=32] {'expert'}, use_global_device_ids=true, to_apply=%region_5.6 | all-reduce | flops 128 | bytes 1024 | tf_op jit(solution)/shard_map/psum | solution.py:89
  615.3 0.5 log_subtract_fusion
  (31 shorter events, 0.1 us)
Async XLA Ops:
  7.2 511.3 %copy-start = (bf16[128,5120]{1,0:T(8,128)(2,1)S(1)}, bf16[128,5120]{1,0:T(8,128)(2,1)}, u32[]{:S(2)}) copy-start(bf16[128,5120]{1,0:T(8,128)(2,1)} %param.20) | copy-start | bytes 3932164
  7.2 145.9 %all-gather.7.cloned.1.call-start = ((), (), s32[]{:S(2)}) async-start(), calls=%async_computation.3 | async-start | bytes 10813440 | tf_op jit(solution)/shard_map/all_gather | solution.py:50
  8.4 3.8 copy-start.10
  12.6 140.5 %copy-start.3 = (bf16[1,48,5120]{2,1,0:T(8,128)(2,1)S(1)}, bf16[1,48,5120]{2,1,0:T(8,128)(2,1)}, u32[]{:S(2)}) copy-start(bf16[1,48,5120]{2,1,0:T(8,128)(2,1)} %param.14) | copy-start | bytes 1474564
  42.6 116.5 %copy-start.4 = (bf16[1,48,5120]{2,1,0:T(8,128)(2,1)S(1)}, bf16[1,48,5120]{2,1,0:T(8,128)(2,1)}, u32[]{:S(2)}) copy-start(bf16[1,48,5120]{2,1,0:T(8,128)(2,1)} %param.15) | copy-start | bytes 1474564
  42.6 199.7 %all-gather.9.cloned.1.call-start = ((), (), s32[]{:S(2)}) async-start(), calls=%async_computation.4 | async-start | bytes 3244032 | tf_op jit(solution)/shard_map/all_gather | solution.py:63
  153.1 7.0 %copy-start.1 = (bf16[1024,5120]{0,1:T(8,128)(2,1)S(1)}, bf16[1024,5120]{0,1:T(8,128)(2,1)}, u32[]{:S(2)}) copy-start(bf16[1024,5120]{0,1:T(8,128)(2,1)} %all-gather.7.cloned.1.call-done) | copy-start | bytes 31457284
  160.1 3.4 copy-start.13
  162.7 160.8 %all-gather.5.cloned.1.call-start = ((), (), s32[]{:S(2)}) async-start(), calls=%async_computation.2 | async-start | bytes 1351680 | tf_op jit(solution)/shard_map/all_gather | solution.py:51
  163.6 78.8 %copy-start.8 = (bf16[1,1536,160]{1,2,0:T(8,128)(2,1)S(1)}, bf16[1,1536,160]{1,2,0:T(8,128)(2,1)}, u32[]{:S(2)}) copy-start(bf16[1,1536,160]{1,2,0:T(8,128)(2,1)} %param.16) | copy-start | bytes 1474564
  250.3 73.2 %copy-start.6 = (bf16[48,5120]{1,0:T(8,128)(2,1)S(1)}, bf16[48,5120]{1,0:T(8,128)(2,1)}, u32[]{:S(2)}) copy-start(bf16[48,5120]{1,0:T(8,128)(2,1)} %param.17) | copy-start | bytes 1474564
  251.9 73.5 %copy-start.7 = (bf16[48,5120]{1,0:T(8,128)(2,1)S(1)}, bf16[48,5120]{1,0:T(8,128)(2,1)}, u32[]{:S(2)}) copy-start(bf16[48,5120]{1,0:T(8,128)(2,1)} %param.18) | copy-start | bytes 1474564
  251.9 110.4 %all-to-all-start.1 = ((bf16[16,2,5120]{2,1,0:T(2,128)(2,1)}), bf16[16,2,5120]{2,1,0:T(2,128)(2,1)S(1)}, u32[]{:S(2)}, u32[]{:S(2)}) async-start(bf16[16,2,5120]{2,1,0:T(2,128)(2,1)} %reshape.84), calls=%async_computation.1 | async-start | bytes 655360 | tf_op jit(solution)/shard_map/all_to_all | solution.py:70
  323.6 1.8 copy-start.2
  363.2 1.2 copy-start.5
  363.2 2.4 copy-start.9
  363.2 2.4 copy-start.11
  365.8 150.0 %copy-start.12 = (bf16[128,160]{0,1:T(8,128)(2,1)}, bf16[128,160]{0,1:T(8,128)(2,1)S(1)}, u32[]{:S(2)}) copy-start(bf16[128,160]{0,1:T(8,128)(2,1)S(1)} %fusion.4) | copy-start | bytes 122884
  516.7 1.7 copy-start.14
Sparse Core Ops, SparseCore 0:
  42.8 110.3 all-gather.6
  162.9 79.4 all-gather.8
  245.5 78.0 all-gather.4
